TPU v7x, 768 devices: a whole 4x8x12 slice. The times are simulated.
768 devices in a mesh: pipe: 24 (over x_lo, z), zero: 32 (over y, x_hi, core).
Axes of the slice: x: 4 (x_hi: 2, x_lo: 2; x = x_hi * 2 + x_lo), y: 8, z: 12, core: 2. Of those that a mesh axis runs over, the one named last changes fastest.
Arguments:
- down_out: bfloat16 [24, 256, 2048], P('pipe', 'zero'), may hold values from -6 to 6
- up_out: bfloat16 [24, 256, 2048], P('pipe', 'zero'), may hold values from -6 to 6
- feeds: bfloat16 [2, 256, 2048], P(None, 'zero'), may hold values from -6 to 6
- order: int32 [2], replicated, may hold values from 0 to 1, each once
- gains: float32 [24, 2, 2048], P('pipe'), may hold values from 0.1 to 1.9
- gate_w: bfloat16 [24, 2, 2048, 4096], P('pipe', None, None, 'zero'), may hold values from -0.125 to 0.125
- up_w: bfloat16 [24, 2, 2048, 4096], P('pipe', None, None, 'zero'), may hold values from -0.125 to 0.125
- down_w: bfloat16 [24, 2, 4096, 2048], P('pipe', None, 'zero'), may hold values from -0.09375 to 0.09375
Outputs:
- down_next: bfloat16 [24, 256, 2048], P('pipe', 'zero')
- up_next: bfloat16 [24, 256, 2048], P('pipe', 'zero')
Inputs may be any that keep to these rules, and one draw needn't show every extreme that they name: `order`: every micro-batch index enters exactly once.
All inputs are finite; a program needn't handle non-finite values.
Results may differ from a plain program's by a relative error of at most 0.02.
Values may be sent and summed in bfloat16 or wider, within the bound.
A program may use at most 32 MiB of HBM per device.

v0:
```python
import jax
import jax.numpy as jnp
from jax import lax
from jax.sharding import PartitionSpec as P

TICKS = 2


def shifted(value, axis, steps):
    count = lax.axis_size(axis)
    first, last = (max(0, -steps), min(count, count - steps))
    return lax.ppermute(value, axis, [(source, source + steps) for source in range(first, last)])


def normalize(x, gain):
    xf = x.astype(jnp.float32)
    return (xf * lax.rsqrt(jnp.mean(xf * xf, axis=-1, keepdims=True) + 1e-05) * gain).astype(
        jnp.bfloat16
    )


def hidden_rows(piece, w_gate, w_up):
    gate = jnp.dot(piece, w_gate, preferred_element_type=jnp.float32)
    up = jnp.dot(piece, w_up, preferred_element_type=jnp.float32)
    return (jax.nn.silu(gate) * up).astype(jnp.bfloat16)


def on_device(down_out, up_out, feeds, order, gains, gate_w, up_w, down_w):
    section = lax.axis_index("pipe")
    first_section = section == 0
    last_section = section == lax.axis_size("pipe") - 1
    down_state = down_out[0]
    up_state = up_out[0]

    def advance(x, slot):
        normed = normalize(x, gains[0, slot])
        hidden = hidden_rows(
            lax.all_gather(normed, "zero", axis=0, tiled=True), gate_w[0, slot], up_w[0, slot]
        )
        summed = lax.psum_scatter(
            jnp.dot(hidden, down_w[0, slot], preferred_element_type=jnp.float32).astype(
                jnp.bfloat16
            ),
            "zero",
            scatter_dimension=0,
            tiled=True,
        ).astype(jnp.float32)
        return (x.astype(jnp.float32) + summed).astype(jnp.bfloat16)

    for tick in range(TICKS):
        arriving = shifted(down_state, "pipe", 1)
        returning = shifted(up_state, "pipe", -1)
        down_in = jnp.where(first_section, feeds[order[tick]], arriving)
        up_in = jnp.where(last_section, down_state, returning)
        down_state = advance(down_in, 0)
        up_state = advance(up_in, 1)
    return (down_state[None], up_state[None])


def solution(mesh):
    return jax.shard_map(
        on_device,
        mesh=mesh,
        in_specs=(
            P("pipe", "zero", None),
            P("pipe", "zero", None),
            P(None, "zero", None),
            P(),
            P("pipe", None, None),
            P("pipe", None, None, "zero"),
            P("pipe", None, None, "zero"),
            P("pipe", None, "zero", None),
        ),
        out_specs=(P("pipe", "zero", None), P("pipe", "zero", None)),
        check_vma=False,
    )
```

profile of v0, /device:TPU:6, one launch (start us, length us, event | category | flops | bytes accessed | tf_op | source)
XLA Modules:
  0.0 932.1 jit_solution(10676167833177116912)
XLA Ops:
  7.2 14.9 %collective-permute-start.2 = (bf16[8,2048]{1,0:T(8,128)(2,1)}, bf16[8,2048]{1,0:T(8,128)(2,1)S(1)}, u32[]{:S(2)}, u32[]{:S(2)}) collective-permute-start(bf16[8,2048]{1,0:T(8,128)(2,1)} %bitcast.65), channel_id=1, source_target_pairs={{32,0},{64,32},{96,64},{128,96},{160,128},{192,160},{224,192},{256... | collective-permute-start | bytes 98312 | tf_op jit(solution)/shard_map/ppermute | solution.py:12
  25.7 1.9 collective-permute-start
  27.7 1.4 fusion.88
  31.0 3.1 collective-permute-done
  35.7 74.2 %all-gather.9.cloned.1.call-done = bf16[256,2048]{1,0:T(8,128)(2,1)} async-done(((bf16[8,2048]{1,0:T(8,128)(2,1)}), bf16[256,2048]{1,0:T(8,128)(2,1)}) %all-gather.9.cloned.1.call-update) | async-done | bytes 1048592 | tf_op jit(solution)/shard_map/all_gather | solution.py:38
  110.0 1.8 fusion.12
  111.8 3.0 convolution_convert_fusion.1
  114.8 85.4 %all-gather.5.cloned.1.call-done = bf16[256,2048]{1,0:T(8,128)(2,1)} async-done(((bf16[8,2048]{1,0:T(8,128)(2,1)}), bf16[256,2048]{1,0:T(8,128)(2,1)}) %all-gather.5.cloned.1.call-update) | async-done | bytes 1048592 | tf_op jit(solution)/shard_map/all_gather | solution.py:38
  200.2 1.9 fusion.22
  202.1 1.8 convolution_convert_fusion.3
  203.9 131.5 %reduce-scatter.9.cloned.1.call-done = bf16[8,2048]{1,0:T(8,128)(2,1)} async-done(((bf16[256,2048]{1,0:T(8,128)(2,1)}), bf16[8,2048]{1,0:T(8,128)(2,1)}) %reduce-scatter.9.cloned.1.call-update) | async-done | bytes 32784 | tf_op jit(solution)/shard_map/reduce_scatter | solution.py:40
  336.2 6.8 collective-permute-start.3
  343.0 128.4 %reduce-scatter.5.cloned.1.call-done = bf16[8,2048]{1,0:T(8,128)(2,1)} async-done(((bf16[256,2048]{1,0:T(8,128)(2,1)}), bf16[8,2048]{1,0:T(8,128)(2,1)}) %reduce-scatter.5.cloned.1.call-update) | async-done | bytes 32784 | tf_op jit(solution)/shard_map/reduce_scatter | solution.py:40
  473.0 3.6 collective-permute-start.1
  478.7 3.1 collective-permute-done.1
  482.7 79.8 %all-gather.11.cloned.1.call-done = bf16[256,2048]{1,0:T(8,128)(2,1)} async-done(((bf16[8,2048]{1,0:T(8,128)(2,1)}), bf16[256,2048]{1,0:T(8,128)(2,1)}) %all-gather.11.cloned.1.call-update) | async-done | bytes 1048592 | tf_op jit(solution)/shard_map/all_gather | solution.py:38
  562.5 1.9 fusion.10
  564.4 1.8 convolution_convert_fusion
  566.2 86.4 %all-gather.7.cloned.1.call-done = bf16[256,2048]{1,0:T(8,128)(2,1)} async-done(((bf16[8,2048]{1,0:T(8,128)(2,1)}), bf16[256,2048]{1,0:T(8,128)(2,1)}) %all-gather.7.cloned.1.call-update) | async-done | bytes 1048592 | tf_op jit(solution)/shard_map/all_gather | solution.py:38
  652.6 1.9 fusion.20
  654.4 1.8 convolution_convert_fusion.2
  656.2 131.4 %reduce-scatter.11.cloned.1.call-done = bf16[8,2048]{1,0:T(8,128)(2,1)} async-done(((bf16[256,2048]{1,0:T(8,128)(2,1)}), bf16[8,2048]{1,0:T(8,128)(2,1)}) %reduce-scatter.11.cloned.1.call-update) | async-done | bytes 32784 | tf_op jit(solution)/shard_map/reduce_scatter | solution.py:40
  787.7 1.4 fusion.80
  789.1 134.8 %reduce-scatter.7.cloned.1.call-done = bf16[8,2048]{1,0:T(8,128)(2,1)} async-done(((bf16[256,2048]{1,0:T(8,128)(2,1)}), bf16[8,2048]{1,0:T(8,128)(2,1)}) %reduce-scatter.7.cloned.1.call-update) | async-done | bytes 32784 | tf_op jit(solution)/shard_map/reduce_scatter | solution.py:40
  (45 shorter events, 10.2 us)
Async XLA Ops:
  7.2 102.8 %all-gather.9.cloned.1.call-start = ((), (), s32[]{:S(2)}) async-start(), calls=%async_computation.8 | async-start | bytes 1081344 | tf_op jit(solution)/shard_map/all_gather | solution.py:38
  7.2 16.8 %collective-permute-start.2 = (bf16[8,2048]{1,0:T(8,128)(2,1)}, bf16[8,2048]{1,0:T(8,128)(2,1)S(1)}, u32[]{:S(2)}, u32[]{:S(2)}) collective-permute-start(bf16[8,2048]{1,0:T(8,128)(2,1)} %bitcast.65), channel_id=1, source_target_pairs={{32,0},{64,32},{96,64},{128,96},{160,128},{192,160},{224,192},{256... | collective-permute-start | bytes 98312 | tf_op jit(solution)/shard_map/ppermute | solution.py:12
  24.0 87.8 %copy-start.1 = (bf16[1,2,2048,128]{3,2,1,0:T(8,128)(2,1)S(1)}, bf16[1,2,2048,128]{3,2,1,0:T(8,128)(2,1)}, u32[]{:S(2)}) copy-start(bf16[1,2,2048,128]{3,2,1,0:T(8,128)(2,1)} %param.14) | copy-start | bytes 3145732
  24.9 86.8 %copy-start = (bf16[1,2,128,2048]{3,2,1,0:T(8,128)(2,1)S(1)}, bf16[1,2,128,2048]{3,2,1,0:T(8,128)(2,1)}, u32[]{:S(2)}) copy-start(bf16[1,2,128,2048]{3,2,1,0:T(8,128)(2,1)} %param.15) | copy-start | bytes 3145732
  25.7 174.5 %all-gather.5.cloned.1.call-start = ((), (), s32[]{:S(2)}) async-start(), calls=%async_computation.4 | async-start | bytes 1081344 | tf_op jit(solution)/shard_map/all_gather | solution.py:38
  25.7 8.3 collective-permute-start
  35.7 299.7 %reduce-scatter.9.cloned.1.call-start = ((), (), s32[]{:S(2)}) async-start(), calls=%async_computation.9 | async-start | bytes 1081344 | tf_op jit(solution)/shard_map/reduce_scatter | solution.py:40
  114.8 356.6 %reduce-scatter.5.cloned.1.call-start = ((), (), s32[]{:S(2)}) async-start(), calls=%async_computation.5 | async-start | bytes 1081344 | tf_op jit(solution)/shard_map/reduce_scatter | solution.py:40
  200.2 1.9 copy-start.3
  203.8 277.9 %copy-start.5 = (bf16[2,8,2048]{2,1,0:T(8,128)(2,1)S(1)}, bf16[2,8,2048]{2,1,0:T(8,128)(2,1)}, u32[]{:S(2)}) copy-start(bf16[2,8,2048]{2,1,0:T(8,128)(2,1)} %param.10) | copy-start | bytes 196612
  203.9 358.6 %all-gather.11.cloned.1.call-start = ((), (), s32[]{:S(2)}) async-start(), calls=%async_computation.10 | async-start | bytes 1081344 | tf_op jit(solution)/shard_map/all_gather | solution.py:38
  336.2 135.2 %collective-permute-start.3 = (bf16[8,2048]{1,0:T(8,128)(2,1)S(1)}, bf16[8,2048]{1,0:T(8,128)(2,1)S(1)}, u32[]{:S(2)}, u32[]{:S(2)}) collective-permute-start(bf16[8,2048]{1,0:T(8,128)(2,1)S(1)} %fusion.71), channel_id=1, source_target_pairs={{32,0},{64,32},{96,64},{128,96},{160,128},{192,160},{224,192},{256... | collective-permute-start | bytes 98312 | tf_op jit(solution)/shard_map/ppermute | solution.py:12
  473.0 179.6 %all-gather.7.cloned.1.call-start = ((), (), s32[]{:S(2)}) async-start(), calls=%async_computation.6 | async-start | bytes 1081344 | tf_op jit(solution)/shard_map/all_gather | solution.py:38
  473.0 8.7 collective-permute-start.1
  482.6 305.1 %reduce-scatter.11.cloned.1.call-start = ((), (), s32[]{:S(2)}) async-start(), calls=%async_computation.11 | async-start | bytes 1081344 | tf_op jit(solution)/shard_map/reduce_scatter | solution.py:40
  562.5 1.9 copy-start.2
  566.1 357.7 %reduce-scatter.7.cloned.1.call-start = ((), (), s32[]{:S(2)}) async-start(), calls=%async_computation.7 | async-start | bytes 1081344 | tf_op jit(solution)/shard_map/reduce_scatter | solution.py:40
  652.6 1.9 copy-start.4
Sparse Core Ops, SparseCore 0:
  25.8 84.1 all-gather.8
  114.5 85.6 all-gather.4
  205.4 129.8 reduce-scatter.8
  340.5 130.8 reduce-scatter.4
  475.7 86.6 all-gather.10
  566.9 85.6 all-gather.6
  657.8 129.8 reduce-scatter.10
  792.9 130.9 reduce-scatter.6
where the time goes:
time: 934 us; the launch traced here: 932 us
  waiting for transfers between devices  859 us (92%)
  starting transfers between devices  27.5 us (3%)
  between operations  18.3 us (2%)
  matrix products  15.6 us (2%)
    reduce_scatter x4, waiting for transfers between devices, advance(): lax.psum_scatter(jnp.dot(hidden, down_w[0, slot], preferred_element_type=...  526 us
    all_gather x4, waiting for transfers between devices, advance(): lax.all_gather(normed, 'zero', axis=0, tiled=True)  326 us
    ppermute x4, starting transfers between devices, shifted(): lax.ppermute(value, axis, [(source, source + steps) for source in range(f...  27.1 us
  transfers between devices with their start and end apart: 12, of which 11 were waited for; matrix products, arithmetic and copies ran while one was open for 2% of the time, Pallas kernels for 0%

commit v1 on v0

v1 whole, which is shorter than its diff:
```python
import functools

import jax
import jax.numpy as jnp
from jax import lax
from jax.experimental import pallas as pl
from jax.experimental.pallas import tpu as pltpu
from jax.sharding import PartitionSpec as P

MESH = pl.DeviceIdType.MESH
TICKS = 2
RING = 8
ROWS = 8

SLOTS = (
    (0, 0), (1, 0), (0, 1), (0, 7),
    (0, 2), (0, 6), (1, 1), (1, 7),
    (0, 3), (0, 5), (1, 2), (1, 6),
    (0, 4), (1, 3), (1, 5), (1, 4),
)
SLOT = {pair: index for index, pair in enumerate(SLOTS)}
UP_REACH = (4, 3)

GATHER = {}
REDUCE = {}
count = 0
for b, d in SLOTS[1:]:
    GATHER[b, d] = count
    count += 1
PAIR_GATHER = count
count += 16
PAIR_REDUCE = count
count += 4
for b in range(2):
    for way in range(2):
        reach = UP_REACH[b] if way == 0 else 7 - UP_REACH[b]
        for hop in range(reach):
            REDUCE[b, way, hop] = count
            count += 1
CROSS = count
SHIFT = count + 1
COPIES = count + 2


def kernel(n_pipe, down_ref, up_ref, feeds_ref, order_ref, gains_ref, gate_ref, upw_ref, downw_ref,
           out_down, out_up,
           wgu, wd, gain_v, feed_v, local_v, xin, xs, ag, part, pair_out, pair_in, run_out, run_in, cross_out, cross_in,
           y_buf, send_sem, recv_sem, load_sem):
    p = lax.axis_index("pipe")
    q = lax.axis_index("zero")
    d_model = wgu.shape[1]
    ahead = (p, lax.rem(q + 4, 32))
    behind = (p, lax.rem(q + 28, 32))
    across = (p, q + 2 - 4 * lax.rem(q // 2, 2))
    partner = (p, q + 1 - 2 * lax.rem(q, 2))
    later = (lax.rem(p + 1, n_pipe), q)
    earlier = (lax.rem(p + n_pipe - 1, n_pipe), q)

    loads = []

    def load(src, dst):
        copy = pltpu.make_async_copy(src, dst, load_sem.at[len(loads)])
        copy.start()
        loads.append(copy)

    load(feeds_ref, feed_v)
    load(down_ref, local_v)
    load(gains_ref, gain_v)
    for g in range(2):
        load(gate_ref.at[0, g], wgu.at[g, :, pl.ds(0, 128)])
        load(upw_ref.at[0, g], wgu.at[g, :, pl.ds(128, 128)])
        load(downw_ref.at[0, g], wd.at[g])

    barrier = pltpu.get_barrier_semaphore()
    for device in (ahead, behind, across, partner, later, earlier):
        pl.semaphore_signal(barrier, inc=1, device_id=device, device_id_type=MESH)
    pl.semaphore_wait(barrier, 6)

    def remote(t, g, number, src, dst, device):
        index = (t * 2 + g) * COPIES + number
        return pltpu.make_async_remote_copy(
            src_ref=src, dst_ref=dst, send_sem=send_sem.at[index], recv_sem=recv_sem.at[index],
            device_id=device, device_id_type=MESH)

    sent = []

    def send(*args):
        copy = remote(*args)
        copy.start()
        sent.append(copy)

    def arrive(t, g, number, dst):
        remote(t, g, number, dst, dst, partner).wait_recv()

    def place(t, g, b, d, r=0):
        return ag.at[t, g, r, SLOT[b, d]]

    def pass_on(t, g, b, d):
        src = place(t, g, b, d)
        if d == 0:
            if b == 0:
                send(t, g, GATHER[1, 0], src, place(t, g, 1, 0), across)
            send(t, g, GATHER[b, 1], src, place(t, g, b, 1), ahead)
            send(t, g, GATHER[b, 7], src, place(t, g, b, 7), behind)
        elif d < UP_REACH[b]:
            send(t, g, GATHER[b, d + 1], src, place(t, g, b, d + 1), ahead)
        elif d > UP_REACH[b] + 1:
            send(t, g, GATHER[b, d - 1], src, place(t, g, b, d - 1), behind)
        send(t, g, PAIR_GATHER + SLOT[b, d], src, place(t, g, b, d, 1), partner)

    def take(t, g, b, d):
        arrive(t, g, GATHER[b, d], place(t, g, b, d))
        pass_on(t, g, b, d)

    def begin(t, g):
        arrive(t, g, SHIFT, xin.at[t, g])
        arrived = xin[t, g].astype(jnp.float32)
        if g == 0:
            x = jnp.where(p == 0, feed_v[order_ref[t]].astype(jnp.float32), arrived)
        else:
            own = local_v[0] if t == 0 else y_buf[0, 0]
            x = jnp.where(p == n_pipe - 1, own.astype(jnp.float32), arrived)
        xs[t, g] = x.astype(jnp.bfloat16)
        scale = lax.rsqrt(jnp.mean(x * x, axis=-1, keepdims=True) + 1e-05)
        ag[t, g, 0, 0] = (x * scale * gain_v[0, pl.ds(g, 1), :]).astype(jnp.bfloat16)
        pass_on(t, g, 0, 0)

    def multiply(t, g, chunk):
        first = chunk * 4
        for k in range(first, first + 4):
            arrive(t, g, PAIR_GATHER + k, ag.at[t, g, 1, k])
        rows = ag[t, g, :, pl.ds(first, 4)].astype(jnp.float32).reshape(64, d_model).astype(jnp.bfloat16)
        both = jnp.dot(rows, wgu[g], preferred_element_type=jnp.float32)
        gate = both[:, :128]
        hidden = (gate / (1.0 + jnp.exp(-gate)) * both[:, 128:]).astype(jnp.bfloat16)
        width = min(512, d_model)
        for n in range(d_model // width):
            cols = pl.ds(n * width, width)
            product = jnp.dot(hidden, wd[g, :, cols], preferred_element_type=jnp.float32)
            product = product.reshape(2, 4, ROWS, width).astype(jnp.bfloat16)
            part[t, g, pl.ds(first, 4), :, cols] = product[0]
            pair_out[t, g, pl.ds(first, 4), :, cols] = product[1]
        send(t, g, PAIR_REDUCE + chunk, pair_out.at[t, g, pl.ds(first, 4)], pair_in.at[t, g, pl.ds(first, 4)], partner)

    def paired(t, g, chunk):
        arrive(t, g, PAIR_REDUCE + chunk, pair_in.at[t, g, pl.ds(chunk * 4, 4)])

    def own_sum(t, g, b, d):
        k = SLOT[b, d]
        return part[t, g, k].astype(jnp.float32) + pair_in[t, g, k].astype(jnp.float32)

    def run_slot(b, way, hop):
        return REDUCE[b, way, hop] - REDUCE[0, 0, 0]

    def reach_of(b, way):
        return UP_REACH[b] if way == 0 else 7 - UP_REACH[b]

    def distance(b, way, hop):
        return (8 - UP_REACH[b] + hop) if way == 0 else (7 - UP_REACH[b] - hop)

    def relay(t, g, b, way, hop):
        total = own_sum(t, g, b, distance(b, way, hop))
        if hop > 0:
            slot = run_slot(b, way, hop - 1)
            arrive(t, g, REDUCE[b, way, hop - 1], run_in.at[t, g, slot])
            total = total + run_in[t, g, slot].astype(jnp.float32)
        slot = run_slot(b, way, hop)
        run_out[t, g, slot] = total.astype(jnp.bfloat16)
        send(t, g, REDUCE[b, way, hop], run_out.at[t, g, slot], run_in.at[t, g, slot], ahead if way == 0 else behind)

    def gathered_sum(t, g, b):
        total = own_sum(t, g, b, 0)
        for way in range(2):
            hop = reach_of(b, way) - 1
            slot = run_slot(b, way, hop)
            arrive(t, g, REDUCE[b, way, hop], run_in.at[t, g, slot])
            total = total + run_in[t, g, slot].astype(jnp.float32)
        return total

    def cross(t, g):
        cross_out[t, g] = gathered_sum(t, g, 1).astype(jnp.bfloat16)
        send(t, g, CROSS, cross_out.at[t, g], cross_in.at[t, g], across)

    def finish(t, g):
        total = gathered_sum(t, g, 0)
        arrive(t, g, CROSS, cross_in.at[t, g])
        total = total + cross_in[t, g].astype(jnp.float32)
        y = (xs[t, g].astype(jnp.float32) + total).astype(jnp.bfloat16)
        if t + 1 < TICKS:
            y_buf[t, g] = y
            send(t + 1, g, SHIFT, y_buf.at[t, g], xin.at[t + 1, g], later if g == 0 else earlier)
        elif g == 0:
            out_down[0] = y
        else:
            out_up[0] = y

    send(0, 0, SHIFT, down_ref.at[0], xin.at[0, 0], later)
    send(0, 1, SHIFT, up_ref.at[0], xin.at[0, 1], earlier)
    for copy in loads[:3]:
        copy.wait()
    for t in range(TICKS):
        for g in range(2):
            begin(t, g)
        for stage, blocks in enumerate((
            ((0, 1), (0, 7)), ((1, 0),), ((0, 2), (0, 6)), ((1, 1), (1, 7)),
            ((0, 3), (0, 5)), ((1, 2), (1, 6)), ((0, 4),), ((1, 3), (1, 5)), ((1, 4),),
        )):
            for g in range(2):
                for b, d in blocks:
                    take(t, g, b, d)
            if t == 0 and stage == 2:
                for copy in loads[3:]:
                    copy.wait()
            if stage in (3, 5, 7):
                for g in range(2):
                    multiply(t, g, (stage - 3) // 2)
        for g in range(2):
            for chunk in range(3):
                paired(t, g, chunk)
            relay(t, g, 0, 1, 0)
        for g in range(2):
            multiply(t, g, 3)
        for g in range(2):
            paired(t, g, 3)
            relay(t, g, 1, 1, 0)
            relay(t, g, 1, 0, 0)
            relay(t, g, 0, 0, 0)
        for hop in range(1, 4):
            for g in range(2):
                for b, way in ((1, 1), (1, 0), (0, 0), (0, 1)):
                    if hop < reach_of(b, way):
                        relay(t, g, b, way, hop)
        for g in range(2):
            cross(t, g)
        for g in range(2):
            finish(t, g)
    for copy in sent:
        copy.wait_send()


def solution(mesh):
    n_pipe = mesh.shape["pipe"]

    def on_device(down_out, up_out, feeds, order, gains, gate_w, up_w, down_w):
        d_model = down_out.shape[-1]
        half = jnp.bfloat16
        block = jax.ShapeDtypeStruct((1, ROWS, d_model), half)
        anywhere = pl.BlockSpec(memory_space=pl.ANY)
        vmem = pl.BlockSpec(memory_space=pltpu.VMEM)
        runs = (TICKS, 2)
        return pl.pallas_call(
            functools.partial(kernel, n_pipe),
            out_shape=(block, block),
            in_specs=[anywhere] * 3 + [pl.BlockSpec(memory_space=pltpu.SMEM)] + [anywhere] * 4,
            out_specs=(vmem, vmem),
            scratch_shapes=[
                pltpu.VMEM((2, d_model, 256), half),
                pltpu.VMEM((2, 128, d_model), half),
                pltpu.VMEM((1, 2, d_model), jnp.float32),
                pltpu.VMEM((TICKS, ROWS, d_model), half),
                pltpu.VMEM((1, ROWS, d_model), half),
                pltpu.VMEM(runs + (ROWS, d_model), half),
                pltpu.VMEM(runs + (ROWS, d_model), half),
                pltpu.VMEM(runs + (2, 16, ROWS, d_model), half),
                pltpu.VMEM(runs + (16, ROWS, d_model), half),
                pltpu.VMEM(runs + (16, ROWS, d_model), half),
                pltpu.VMEM(runs + (16, ROWS, d_model), half),
                pltpu.VMEM(runs + (14, ROWS, d_model), half),
                pltpu.VMEM(runs + (14, ROWS, d_model), half),
                pltpu.VMEM(runs + (ROWS, d_model), half),
                pltpu.VMEM(runs + (ROWS, d_model), half),
                pltpu.VMEM((TICKS - 1, 2, ROWS, d_model), half),
                pltpu.SemaphoreType.DMA((TICKS * 2 * COPIES,)),
                pltpu.SemaphoreType.DMA((TICKS * 2 * COPIES,)),
                pltpu.SemaphoreType.DMA((9,)),
            ],
            compiler_params=pltpu.CompilerParams(
                collective_id=0, has_side_effects=True, vmem_limit_bytes=60 * 1024 * 1024),
        )(down_out, up_out, feeds, order, gains, gate_w, up_w, down_w)

    return jax.shard_map(
        on_device,
        mesh=mesh,
        in_specs=(
            P("pipe", "zero", None),
            P("pipe", "zero", None),
            P(None, "zero", None),
            P(),
            P("pipe", None, None),
            P("pipe", None, None, "zero"),
            P("pipe", None, None, "zero"),
            P("pipe", None, "zero", None),
        ),
        out_specs=(P("pipe", "zero", None), P("pipe", "zero", None)),
        check_vma=False,
    )
```

time: 934 us -> 109 us (0.12)
  waiting for transfers between devices: 859 us -> 0 us
  Pallas kernels: 0 us -> 105 us
  starting transfers between devices: 27.5 us -> 0 us
  between operations: 18.3 us -> 0.65 us
  matrix products: 15.6 us -> 0 us
    reduce_scatter x4 -> x0, waiting for transfers between devices: 526 us -> none  [advance(): lax.psum_scatter(jnp.dot(hidden, down_w[0, slot], preferred_element_type=...]
    all_gather x4 -> x0, waiting for transfers between devices: 326 us -> none  [advance(): lax.all_gather(normed, 'zero', axis=0, tiled=True)]
    pallas_call x0 -> x1, Pallas kernels: none -> 105 us  [on_device(): pl.pallas_call(functools.partial(kernel, n_pipe), out_shape=(block, block...]
    ppermute x4 -> x0, starting transfers between devices: 27.1 us -> none  [shifted(): lax.ppermute(value, axis, [(source, source + steps) for source in range(f...]
    dot_general x8 -> x0, matrix products: 15.6 us -> none  [the longest x4 8.26 us: advance(): jnp.dot(hidden, down_w[0, slot], preferred_element_type=jnp.float32)]
  transfers between devices with their start and end apart: 12 -> 0, of which waited for: 11 -> 0; matrix products, arithmetic and copies ran while one was open for 2% -> 0% of each run, Pallas kernels for 0% -> 0%
where the time goes in v1:
time: 109 us; the launch traced here: 108 us
  Pallas kernels  105 us (96%)
  local copies, waits for them, and re-layouts  2 us (2%)
    pallas_call x1, Pallas kernels, on_device(): pl.pallas_call(functools.partial(kernel, n_pipe), out_shape=(block, block...  105 us

profile of v1, /device:TPU:6, one launch (start us, length us, event | category | flops | bytes accessed | tf_op | source)
XLA Modules:
  0.0 107.7 jit_solution(15751337064171834410)
XLA Ops:
  0.6 105.1 %shard_map.95 = (bf16[1,8,2048]{2,1,0:T(8,128)(2,1)}, bf16[1,8,2048]{2,1,0:T(8,128)(2,1)}) custom-call(bf16[1,8,2048]{2,1,0:T(8,128)(2,1)} %down_ref.1, bf16[1,8,2048]{2,1,0:T(8,128)(2,1)} %up_ref.1, bf16[2,8,2048]{2,1,0:T(8,128)(2,1)} %feeds_ref.1, s32[2]{0:T(128)} %order_ref.1, f32[1,2,2048]{2,1,0:T(2,128)} %gains_ref.1, ...), custom_call_target="tpu_custom_call" | custom-call | tf_op jit(solution)/shard_map/pallas_call | solution.py:251
  105.7 0.0 copy-start
  105.7 1.4 %copy.12 = bf16[1,8,2048]{2,1,0:T(8,128)(2,1)} copy(bf16[1,8,2048]{2,1,0:T(8,128)(2,1)} %get-tuple-element.4) | data formatting | bytes 65536
  107.1 0.0 copy-done
  107.1 0.6 copy.13
Async XLA Ops:
  105.7 1.4 %copy-start = (bf16[1,8,2048]{2,1,0:T(8,128)(2,1)S(1)}, bf16[1,8,2048]{2,1,0:T(8,128)(2,1)}, u32[]{:S(2)}) copy-start(bf16[1,8,2048]{2,1,0:T(8,128)(2,1)} %get-tuple-element.5) | copy-start | bytes 98308

commit v2 on v0

v2 whole, which is shorter than its diff:
```python
import functools

import jax
import jax.numpy as jnp
from jax import lax
from jax.experimental import pallas as pl
from jax.experimental.pallas import tpu as pltpu
from jax.sharding import PartitionSpec as P

MESH = pl.DeviceIdType.MESH
TICKS = 2
ROWS = 8

BLOCKS = (
    (0, 0), (0, 1), (0, 7), (0, 2), (0, 6), (1, 0),
    (0, 3), (0, 5), (1, 2), (1, 6), (1, 1),
    (1, 7), (0, 4), (1, 3), (1, 5), (1, 4),
)
CHUNKS = ((0, 6), (6, 5), (11, 5))
SLOT = {block: index for index, block in enumerate(BLOCKS)}
PARENT = {
    (0, 2): (0, 0), (0, 6): (0, 0), (1, 0): (0, 0), (0, 1): (0, 0), (0, 7): (0, 0),
    (1, 3): (0, 2), (0, 4): (0, 2), (1, 2): (0, 2), (0, 3): (0, 2),
    (1, 4): (0, 6), (1, 5): (0, 6), (1, 6): (0, 6), (0, 5): (0, 6),
    (1, 1): (1, 0), (1, 7): (1, 0),
}
CHILDREN = {block: [child for child, parent in PARENT.items() if parent == block] for block in BLOCKS}
RELAYS = [block for block in BLOCKS[1:] if CHILDREN[block]]
LEAVES = [block for block in BLOCKS[1:] if not CHILDREN[block]]

PAIR_GATHER = 16
PAIR_REDUCE = 19
REDUCE = 22
SUMS = {block: REDUCE + index for index, block in enumerate([(0, 0)] + RELAYS)}
ARRIVALS = REDUCE + len(SUMS)
RELAYED, PAIRED, PARTIALS, SUMMED, LAUNCHED, SHIFTED = range(6)
KINDS = 6


def step_of(child, parent):
    return child[0] ^ parent[0], (child[1] - parent[1] + 4) % 8 - 4


def kernel(n_pipe, down_ref, up_ref, feeds_ref, order_ref, gains_ref, gate_ref, upw_ref, downw_ref,
           out_down, out_up,
           wgu, wd, gain_v, feed_v, first, ag, part, pair_out, pair_in, run_out, run_in, y_buf,
           send_sem, recv_sem, load_sem):
    scope = jax.named_scope
    p = lax.axis_index("pipe")
    q = lax.axis_index("zero")
    d_model = wgu.shape[1]
    opposite = q + 2 - 4 * lax.rem(q // 2, 2)

    def device(plane, flip, steps):
        return (plane, lax.rem((opposite if flip else q) + 4 * (steps % 8), 32))

    partner = (p, q + 1 - 2 * lax.rem(q, 2))
    is_first = p == 0
    is_last = p == n_pipe - 1
    stays = (is_last, is_first)

    loads = []

    def load(src, dst):
        copy = pltpu.make_async_copy(src, dst, load_sem.at[len(loads)])
        copy.start()
        loads.append(copy)

    load(feeds_ref, feed_v)
    load(down_ref.at[0], first.at[0])
    load(up_ref.at[0], first.at[1])
    load(gains_ref, gain_v)
    for g in range(2):
        load(gate_ref.at[0, g], wgu.at[g, :, pl.ds(0, 128)])
        load(upw_ref.at[0, g], wgu.at[g, :, pl.ds(128, 128)])
        load(downw_ref.at[0, g], wd.at[g])

    barrier = pltpu.get_barrier_semaphore()
    near = {step_of(child, parent) for child, parent in PARENT.items()}
    near = sorted(near | {(flip, -steps) for flip, steps in near})
    roots = sorted({(0, 0)} | {step_of(child, (0, 0)) for child in CHILDREN[0, 0]})
    meets = [partner] + [device(p, *step) for step in near]
    barrier_count = len(meets) + jnp.where(is_first, 0, len(roots)) + jnp.where(is_last, 0, len(roots))
    with scope("barr"):
        for other in meets:
            pl.semaphore_signal(barrier, inc=1, device_id=other, device_id_type=MESH)

        @pl.when(jnp.logical_not(is_last))
        def _():
            for step in roots:
                pl.semaphore_signal(barrier, inc=1, device_id=device(p + 1, *step), device_id_type=MESH)

        @pl.when(jnp.logical_not(is_first))
        def _():
            for step in roots:
                pl.semaphore_signal(barrier, inc=1, device_id=device(p - 1, *step), device_id_type=MESH)

        pl.semaphore_wait(barrier, barrier_count)

    def leaving(t, g, kind):
        return send_sem.at[(t * 2 + g) * KINDS + kind]

    def arriving(t, g, number):
        return recv_sem.at[(t * 2 + g) * ARRIVALS + number]

    def remote(src, dst, out_sem, in_sem, device):
        return pltpu.make_async_remote_copy(
            src_ref=src, dst_ref=dst, send_sem=out_sem, recv_sem=in_sem, device_id=device, device_id_type=MESH)

    def arrive(t, g, number, dst):
        remote(dst, dst, leaving(t, g, 0), arriving(t, g, number), partner).wait_recv()

    def place(t, g, block, r=0):
        return ag.at[t, g, r, SLOT[block]]

    def launch(t, stream, src, plane, g, stays):
        for child in CHILDREN[0, 0][:2] + [(0, 0)] + CHILDREN[0, 0][2:]:
            kind = SHIFTED if child == (0, 0) else LAUNCHED
            copy = remote(src, place(t, g, child), leaving(t, stream, kind), arriving(t, g, SLOT[child]),
                          device(plane, *step_of(child, (0, 0))))
            if child == (0, 0):
                pl.when(jnp.logical_not(stays))(copy.start)
                own = pltpu.make_async_copy(src, place(t, g, child), arriving(t, g, SLOT[child]))
                pl.when(stays)(own.start)
            else:
                copy.start()

    def launch_down(t, src):
        launch(t, 0, src, jnp.where(is_last, p, p + 1), jnp.where(is_last, 1, 0), is_last)

        @pl.when(is_first)
        def _():
            y_buf[t, 1] = feed_v[order_ref[t]]
            launch(t, 1, y_buf.at[t, 1], p, 0, is_first)

    def launch_up(t, src):
        @pl.when(jnp.logical_not(is_first))
        def _():
            launch(t, 1, src, p - 1, 1, is_first)

    def take(t, g, block):
        src = place(t, g, block)
        arrive(t, g, SLOT[block], src)
        if block != (0, 0):
            for child in CHILDREN[block]:
                remote(src, place(t, g, child), leaving(t, g, RELAYED), arriving(t, g, SLOT[child]),
                       device(p, *step_of(child, block))).start()
        chunk = sum(SLOT[block] >= begin for begin, _ in CHUNKS) - 1
        remote(src, place(t, g, block, 1), leaving(t, g, PAIRED), arriving(t, g, PAIR_GATHER + chunk), partner).start()

    def multiply(t, g, chunk):
        begin, number = CHUNKS[chunk]
        slots = pl.ds(begin, number)
        arrive(t, g, PAIR_GATHER + chunk, ag.at[t, g, 1, slots])
        x = ag[t, g, :, slots].astype(jnp.float32).reshape(2 * number * ROWS, d_model)
        scale = lax.rsqrt(jnp.mean(x * x, axis=-1, keepdims=True) + 1e-05)
        rows = (x * scale * gain_v[0, pl.ds(g, 1), :]).astype(jnp.bfloat16)
        both = jnp.dot(rows, wgu[g], preferred_element_type=jnp.float32)
        gate = both[:, :128]
        hidden = (gate / (1.0 + jnp.exp(-gate)) * both[:, 128:]).astype(jnp.bfloat16)
        width = min(512, d_model)
        for n in range(d_model // width):
            cols = pl.ds(n * width, width)
            product = jnp.dot(hidden, wd[g, :, cols], preferred_element_type=jnp.float32)
            product = product.reshape(2, number, ROWS, width).astype(jnp.bfloat16)
            part[t, g, slots, :, cols] = product[0]
            pair_out[t, g, slots, :, cols] = product[1]
        remote(pair_out.at[t, g, slots], pair_in.at[t, g, slots], leaving(t, g, PARTIALS),
               arriving(t, g, PAIR_REDUCE + chunk), partner).start()

    def total_of(t, g, block):
        k = SLOT[block]
        total = part[t, g, k].astype(jnp.float32) + pair_in[t, g, k].astype(jnp.float32)
        children = CHILDREN[block]
        if children:
            arrive(t, g, SUMS[block], run_in.at[t, g, pl.ds(0, len(children))])
        for child in children:
            total = total + run_in[t, g, SLOT[child]].astype(jnp.float32)
        return total

    def hand_in(t, g, block):
        k = SLOT[block]
        run_out[t, g, k] = total_of(t, g, block).astype(jnp.bfloat16)
        parent = PARENT[block]
        flip, steps = step_of(block, parent)
        remote(run_out.at[t, g, k], run_in.at[t, g, k], leaving(t, g, SUMMED), arriving(t, g, SUMS[parent]),
               device(p, flip, -steps)).start()

    def finish(t, g):
        y = (ag[t, g, 0, 0].astype(jnp.float32) + total_of(t, g, (0, 0))).astype(jnp.bfloat16)
        if t + 1 == TICKS:
            (out_down if g == 0 else out_up)[0] = y
            return
        if g == 0:
            y_buf[t + 1, 0] = y
            launch_down(t + 1, y_buf.at[t + 1, 0])
        else:
            @pl.when(jnp.logical_not(is_first))
            def _():
                y_buf[t + 1, 1] = y
                launch_up(t + 1, y_buf.at[t + 1, 1])

    def enter(t, g):
        with scope(f"L1_{t}{g}"):
            for block in ((0, 2), (0, 6), (1, 0), (0, 0), (0, 1), (0, 7)):
                take(t, g, block)

    def deepen(t, g):
        with scope(f"L2_{t}{g}"):
            for block in BLOCKS[6:]:
                take(t, g, block)

    def work(t, g, chunk):
        with scope(f"M{chunk}_{t}{g}"):
            multiply(t, g, chunk)

    def leaf(t, g, chunk):
        with scope(f"LV{chunk}_{t}{g}"):
            begin, number = CHUNKS[chunk]
            arrive(t, g, PAIR_REDUCE + chunk, pair_in.at[t, g, pl.ds(begin, number)])
            for block in BLOCKS[begin:begin + number]:
                if block in LEAVES:
                    hand_in(t, g, block)

    def relay(t, g):
        with scope(f"RL_{t}{g}"):
            for block in RELAYS:
                hand_in(t, g, block)

    def close(t, g):
        with scope(f"FI_{t}{g}"):
            finish(t, g)

    def start(g):
        with scope(f"GO_{g}"):
            if g == 0:
                launch_down(0, first.at[0])
            else:
                launch_up(0, first.at[1])

    for copy in loads[:3]:
        copy.wait()
    start(0)
    start(1)
    for t in range(TICKS):
        enter(t, 0)
        enter(t, 1)
        if t == 0:
            for copy in loads[3:]:
                copy.wait()
        work(t, 0, 0)
        deepen(t, 0)
        work(t, 1, 0)
        work(t, 0, 1)
        deepen(t, 1)
        work(t, 0, 2)
        leaf(t, 0, 1)
        work(t, 1, 1)
        leaf(t, 0, 2)
        leaf(t, 0, 0)
        work(t, 1, 2)
        leaf(t, 1, 1)
        leaf(t, 1, 0)
        leaf(t, 1, 2)
        relay(t, 0)
        relay(t, 1)
        close(t, 0)
        close(t, 1)
    with scope("drain"):
        for t in range(TICKS):
            for g in range(2):
                for kind, blocks in ((RELAYED, 10), (PAIRED, 16), (PARTIALS, 16), (SUMMED, 15), (LAUNCHED, 5)):
                    ref = ag.at[t, g, 0, pl.ds(0, blocks)]
                    remote(ref, ref, leaving(t, g, kind), arriving(t, g, 0), partner).wait_send()
                ref = ag.at[t, g, 0, 0]
                shift = remote(ref, ref, leaving(t, g, SHIFTED), arriving(t, g, 0), partner)
                pl.when(jnp.logical_not(stays[g]))(shift.wait_send)


def solution(mesh):
    n_pipe = mesh.shape["pipe"]

    def on_device(down_out, up_out, feeds, order, gains, gate_w, up_w, down_w):
        d_model = down_out.shape[-1]
        half = jnp.bfloat16
        block = jax.ShapeDtypeStruct((1, ROWS, d_model), half)
        anywhere = pl.BlockSpec(memory_space=pl.ANY)
        vmem = pl.BlockSpec(memory_space=pltpu.VMEM)
        runs = (TICKS, 2)
        return pl.pallas_call(
            functools.partial(kernel, n_pipe),
            out_shape=(block, block),
            in_specs=[anywhere] * 3 + [pl.BlockSpec(memory_space=pltpu.SMEM)] + [anywhere] * 4,
            out_specs=(vmem, vmem),
            scratch_shapes=[
                pltpu.VMEM((2, d_model, 256), half),
                pltpu.VMEM((2, 128, d_model), half),
                pltpu.VMEM((1, 2, d_model), jnp.float32),
                pltpu.VMEM((TICKS, ROWS, d_model), half),
                pltpu.VMEM((2, ROWS, d_model), half),
                pltpu.VMEM(runs + (2, 16, ROWS, d_model), half),
                pltpu.VMEM(runs + (16, ROWS, d_model), half),
                pltpu.VMEM(runs + (16, ROWS, d_model), half),
                pltpu.VMEM(runs + (16, ROWS, d_model), half),
                pltpu.VMEM(runs + (16, ROWS, d_model), half),
                pltpu.VMEM(runs + (16, ROWS, d_model), half),
                pltpu.VMEM(runs + (ROWS, d_model), half),
                pltpu.SemaphoreType.DMA((TICKS * 2 * KINDS,)),
                pltpu.SemaphoreType.DMA((TICKS * 2 * ARRIVALS,)),
                pltpu.SemaphoreType.DMA((10,)),
            ],
            compiler_params=pltpu.CompilerParams(
                collective_id=0, has_side_effects=True, vmem_limit_bytes=60 * 1024 * 1024),
        )(down_out, up_out, feeds, order, gains, gate_w, up_w, down_w)

    return jax.shard_map(
        on_device,
        mesh=mesh,
        in_specs=(
            P("pipe", "zero", None),
            P("pipe", "zero", None),
            P(None, "zero", None),
            P(),
            P("pipe", None, None),
            P("pipe", None, None, "zero"),
            P("pipe", None, None, "zero"),
            P("pipe", None, "zero", None),
        ),
        out_specs=(P("pipe", "zero", None), P("pipe", "zero", None)),
        check_vma=False,
    )
```

time: 934 us -> 85.6 us (0.09)
  waiting for transfers between devices: 859 us -> 0 us
  Pallas kernels: 0 us -> 82.1 us
  starting transfers between devices: 27.5 us -> 0 us
  between operations: 18.3 us -> 0.65 us
  matrix products: 15.6 us -> 0 us
    reduce_scatter x4 -> x0, waiting for transfers between devices: 526 us -> none  [advance(): lax.psum_scatter(jnp.dot(hidden, down_w[0, slot], preferred_element_type=...]
    all_gather x4 -> x0, waiting for transfers between devices: 326 us -> none  [advance(): lax.all_gather(normed, 'zero', axis=0, tiled=True)]
    pallas_call x0 -> x1, Pallas kernels: none -> 82.1 us  [on_device(): pl.pallas_call(functools.partial(kernel, n_pipe), out_shape=(block, block...]
    ppermute x4 -> x0, starting transfers between devices: 27.1 us -> none  [shifted(): lax.ppermute(value, axis, [(source, source + steps) for source in range(f...]
    dot_general x8 -> x0, matrix products: 15.6 us -> none  [the longest x4 8.26 us: advance(): jnp.dot(hidden, down_w[0, slot], preferred_element_type=jnp.float32)]
  transfers between devices with their start and end apart: 12 -> 0, of which waited for: 11 -> 0; matrix products, arithmetic and copies ran while one was open for 2% -> 0% of each run, Pallas kernels for 0% -> 0%
where the time goes in v2:
time: 85.6 us; the launch traced here: 84.8 us
  Pallas kernels  82.1 us (96%)
  local copies, waits for them, and re-layouts  2 us (2%)
    pallas_call x1, Pallas kernels, on_device(): pl.pallas_call(functools.partial(kernel, n_pipe), out_shape=(block, block...  82.1 us
    unnamed x4, local copies, waits for them, and re-layouts  2 us

profile of v2, /device:TPU:6, one launch (start us, length us, event | category | flops | bytes accessed | tf_op | source)
XLA Modules:
  0.0 84.8 jit_solution(15754484822405299640)
XLA Ops:
  0.6 82.1 %shard_map.95 = (bf16[1,8,2048]{2,1,0:T(8,128)(2,1)}, bf16[1,8,2048]{2,1,0:T(8,128)(2,1)}) custom-call(bf16[1,8,2048]{2,1,0:T(8,128)(2,1)} %down_ref.1, bf16[1,8,2048]{2,1,0:T(8,128)(2,1)} %up_ref.1, bf16[2,8,2048]{2,1,0:T(8,128)(2,1)} %feeds_ref.1, s32[2]{0:T(128)} %order_ref.1, f32[1,2,2048]{2,1,0:T(2,128)} %gains_ref.1, ...), custom_call_target="tpu_custom_call" | custom-call | tf_op jit(solution)/shard_map/pallas_call | solution.py:290
  82.8 0.0 copy-start
  82.8 1.4 %copy.12 = bf16[1,8,2048]{2,1,0:T(8,128)(2,1)} copy(bf16[1,8,2048]{2,1,0:T(8,128)(2,1)} %get-tuple-element.4) | data formatting | bytes 65536
  84.1 0.0 copy-done
  84.1 0.6 copy.13
Async XLA Ops:
  82.8 1.4 %copy-start = (bf16[1,8,2048]{2,1,0:T(8,128)(2,1)S(1)}, bf16[1,8,2048]{2,1,0:T(8,128)(2,1)}, u32[]{:S(2)}) copy-start(bf16[1,8,2048]{2,1,0:T(8,128)(2,1)} %get-tuple-element.5) | copy-start | bytes 98308

commit v3 on v2

--- a/solution.py
+++ b/solution.py
@@ -16,7 +16,7 @@
     (0, 3), (0, 5), (1, 2), (1, 6), (1, 1),
     (1, 7), (0, 4), (1, 3), (1, 5), (1, 4),
 )
-CHUNKS = ((0, 6), (6, 5), (11, 5))
+CHUNKS = ((0, 6), (6, 10))
 SLOT = {block: index for index, block in enumerate(BLOCKS)}
 PARENT = {
     (0, 2): (0, 0), (0, 6): (0, 0), (1, 0): (0, 0), (0, 1): (0, 0), (0, 7): (0, 0),
@@ -29,8 +29,8 @@
 LEAVES = [block for block in BLOCKS[1:] if not CHILDREN[block]]
 
 PAIR_GATHER = 16
-PAIR_REDUCE = 19
-REDUCE = 22
+PAIR_REDUCE = 18
+REDUCE = 20
 SUMS = {block: REDUCE + index for index, block in enumerate([(0, 0)] + RELAYS)}
 ARRIVALS = REDUCE + len(SUMS)
 RELAYED, PAIRED, PARTIALS, SUMMED, LAUNCHED, SHIFTED = range(6)
@@ -41,10 +41,10 @@
     return child[0] ^ parent[0], (child[1] - parent[1] + 4) % 8 - 4
 
 
-def kernel(n_pipe, down_ref, up_ref, feeds_ref, order_ref, gains_ref, gate_ref, upw_ref, downw_ref,
-           out_down, out_up,
+def kernel(n_pipe, down_ref, up_ref, feeds_ref, order_hbm, gains_ref, gate_ref, upw_ref, downw_ref,
+           outs,
            wgu, wd, gain_v, feed_v, first, ag, part, pair_out, pair_in, run_out, run_in, y_buf,
-           send_sem, recv_sem, load_sem):
+           order_ref, out_v, send_sem, recv_sem, load_sem, store_sem):
     scope = jax.named_scope
     p = lax.axis_index("pipe")
     q = lax.axis_index("zero")
@@ -66,6 +66,7 @@
         copy.start()
         loads.append(copy)
 
+    load(order_hbm, order_ref)
     load(feeds_ref, feed_v)
     load(down_ref.at[0], first.at[0])
     load(up_ref.at[0], first.at[1])
@@ -186,10 +187,14 @@
         remote(run_out.at[t, g, k], run_in.at[t, g, k], leaving(t, g, SUMMED), arriving(t, g, SUMS[parent]),
                device(p, flip, -steps)).start()
 
+    def store(g):
+        return pltpu.make_async_copy(out_v.at[g], outs.at[g], store_sem.at[g])
+
     def finish(t, g):
         y = (ag[t, g, 0, 0].astype(jnp.float32) + total_of(t, g, (0, 0))).astype(jnp.bfloat16)
         if t + 1 == TICKS:
-            (out_down if g == 0 else out_up)[0] = y
+            out_v[g] = y
+            store(g).start()
             return
         if g == 0:
             y_buf[t + 1, 0] = y
@@ -238,35 +243,41 @@
             else:
                 launch_up(0, first.at[1])
 
-    for copy in loads[:3]:
+    for copy in loads[:4]:
         copy.wait()
     start(0)
     start(1)
+    enter(0, 0)
+    enter(0, 1)
+    for copy in loads[4:]:
+        copy.wait()
     for t in range(TICKS):
-        enter(t, 0)
-        enter(t, 1)
-        if t == 0:
-            for copy in loads[3:]:
-                copy.wait()
         work(t, 0, 0)
         deepen(t, 0)
-        work(t, 1, 0)
-        work(t, 0, 1)
-        deepen(t, 1)
-        work(t, 0, 2)
+        if t == 0:
+            work(t, 1, 0)
+            work(t, 0, 1)
+            deepen(t, 1)
+        else:
+            enter(t, 1)
+            work(t, 0, 1)
+            work(t, 1, 0)
         leaf(t, 0, 1)
+        leaf(t, 0, 0)
+        if t > 0:
+            deepen(t, 1)
         work(t, 1, 1)
-        leaf(t, 0, 2)
-        leaf(t, 0, 0)
-        work(t, 1, 2)
+        leaf(t, 1, 0)
         leaf(t, 1, 1)
-        leaf(t, 1, 0)
-        leaf(t, 1, 2)
         relay(t, 0)
         relay(t, 1)
         close(t, 0)
+        if t + 1 < TICKS:
+            enter(t + 1, 0)
         close(t, 1)
     with scope("drain"):
+        for g in range(2):
+            store(g).wait()
         for t in range(TICKS):
             for g in range(2):
                 for kind, blocks in ((RELAYED, 10), (PAIRED, 16), (PARTIALS, 16), (SUMMED, 15), (LAUNCHED, 5)):
@@ -283,15 +294,13 @@
     def on_device(down_out, up_out, feeds, order, gains, gate_w, up_w, down_w):
         d_model = down_out.shape[-1]
         half = jnp.bfloat16
-        block = jax.ShapeDtypeStruct((1, ROWS, d_model), half)
         anywhere = pl.BlockSpec(memory_space=pl.ANY)
-        vmem = pl.BlockSpec(memory_space=pltpu.VMEM)
         runs = (TICKS, 2)
-        return pl.pallas_call(
+        both = pl.pallas_call(
             functools.partial(kernel, n_pipe),
-            out_shape=(block, block),
-            in_specs=[anywhere] * 3 + [pl.BlockSpec(memory_space=pltpu.SMEM)] + [anywhere] * 4,
-            out_specs=(vmem, vmem),
+            out_shape=jax.ShapeDtypeStruct((2, ROWS, d_model), half),
+            in_specs=[anywhere] * 8,
+            out_specs=anywhere,
             scratch_shapes=[
                 pltpu.VMEM((2, d_model, 256), half),
                 pltpu.VMEM((2, 128, d_model), half),
@@ -305,13 +314,17 @@
                 pltpu.VMEM(runs + (16, ROWS, d_model), half),
                 pltpu.VMEM(runs + (16, ROWS, d_model), half),
                 pltpu.VMEM(runs + (ROWS, d_model), half),
+                pltpu.SMEM((TICKS,), jnp.int32),
+                pltpu.VMEM((2, ROWS, d_model), half),
                 pltpu.SemaphoreType.DMA((TICKS * 2 * KINDS,)),
                 pltpu.SemaphoreType.DMA((TICKS * 2 * ARRIVALS,)),
-                pltpu.SemaphoreType.DMA((10,)),
+                pltpu.SemaphoreType.DMA((11,)),
+                pltpu.SemaphoreType.DMA((2,)),
             ],
             compiler_params=pltpu.CompilerParams(
                 collective_id=0, has_side_effects=True, vmem_limit_bytes=60 * 1024 * 1024),
         )(down_out, up_out, feeds, order, gains, gate_w, up_w, down_w)
+        return both[:1], both[1:]
 
     return jax.shard_map(
         on_device,

time: 85.6 us -> 82.8 us (0.967)
  Pallas kernels: 82.1 us -> 80.5 us
    unnamed x4 -> x0, local copies, waits for them, and re-layouts: 2 us -> none
    pallas_call x1, Pallas kernels: 82.1 us -> 80.5 us  [on_device(): pl.pallas_call(functools.partial(kernel, n_pipe), out_shape=jax.ShapeDtyp...]
    slice x0 -> x1, local copies, waits for them, and re-layouts: none -> 1.4 us  [on_device(): return (both[:1], both[1:])]
where the time goes in v3:
time: 82.8 us; the launch traced here: 82.5 us
  Pallas kernels  80.5 us (97%)
  local copies, waits for them, and re-layouts  1.4 us (2%)
    pallas_call x1, Pallas kernels, on_device(): pl.pallas_call(functools.partial(kernel, n_pipe), out_shape=jax.ShapeDtyp...  80.5 us

profile of v3, /device:TPU:6, one launch (start us, length us, event | category | flops | bytes accessed | tf_op | source)
XLA Modules:
  0.0 82.5 jit_solution(15490176392615116073)
XLA Ops:
  0.6 80.5 %shard_map.95 = bf16[2,8,2048]{2,1,0:T(8,128)(2,1)} custom-call(bf16[1,8,2048]{2,1,0:T(8,128)(2,1)} %down_ref.1, bf16[1,8,2048]{2,1,0:T(8,128)(2,1)} %up_ref.1, bf16[2,8,2048]{2,1,0:T(8,128)(2,1)} %feeds_ref.1, s32[2]{0:T(128)} %order_hbm.1, f32[1,2,2048]{2,1,0:T(2,128)} %gains_ref.1, bf16[1,2,2048,128]{3,2,1,0:T(8,128)(2,1)} %gate_ref.1, ...), custom_call_target="tpu_custom_call" | custom-call | tf_op jit(solution)/shard_map/pallas_call | solution.py:299
  81.1 1.4 %fusion = (bf16[1,8,2048]{2,1,0:T(8,128)(2,1)}, bf16[1,8,2048]{2,1,0:T(8,128)(2,1)}) fusion(bf16[2,8,2048]{2,1,0:T(8,128)(2,1)} %shard_map.95), kind=kLoop, calls=%fused_computation | loop fusion | bytes 131072 | tf_op jit(solution)/shard_map/slice | solution.py:327

commit v4 on v3

--- a/solution.py
+++ b/solution.py
@@ -223,7 +223,7 @@
         with scope(f"LV{chunk}_{t}{g}"):
             begin, number = CHUNKS[chunk]
             arrive(t, g, PAIR_REDUCE + chunk, pair_in.at[t, g, pl.ds(begin, number)])
-            for block in BLOCKS[begin:begin + number]:
+            for block in reversed(BLOCKS[begin:begin + number]):
                 if block in LEAVES:
                     hand_in(t, g, block)
 

time: 82.8 us -> 82.4 us (level)
  no operation moved by 1% of the time
where the time goes in v4:
time: 82.4 us; the launch traced here: 81.7 us
  Pallas kernels  79.7 us (97%)
  local copies, waits for them, and re-layouts  1.4 us (2%)
    pallas_call x1, Pallas kernels, on_device(): pl.pallas_call(functools.partial(kernel, n_pipe), out_shape=jax.ShapeDtyp...  79.7 us

profile of v4, /device:TPU:6, one launch (start us, length us, event | category | flops | bytes accessed | tf_op | source)
XLA Modules:
  0.0 81.7 jit_solution(18392080526447897632)
XLA Ops:
  0.6 79.7 %shard_map.95 = bf16[2,8,2048]{2,1,0:T(8,128)(2,1)} custom-call(bf16[1,8,2048]{2,1,0:T(8,128)(2,1)} %down_ref.1, bf16[1,8,2048]{2,1,0:T(8,128)(2,1)} %up_ref.1, bf16[2,8,2048]{2,1,0:T(8,128)(2,1)} %feeds_ref.1, s32[2]{0:T(128)} %order_hbm.1, f32[1,2,2048]{2,1,0:T(2,128)} %gains_ref.1, bf16[1,2,2048,128]{3,2,1,0:T(8,128)(2,1)} %gate_ref.1, ...), custom_call_target="tpu_custom_call" | custom-call | tf_op jit(solution)/shard_map/pallas_call | solution.py:299
  80.3 1.4 %fusion = (bf16[1,8,2048]{2,1,0:T(8,128)(2,1)}, bf16[1,8,2048]{2,1,0:T(8,128)(2,1)}) fusion(bf16[2,8,2048]{2,1,0:T(8,128)(2,1)} %shard_map.95), kind=kLoop, calls=%fused_computation | loop fusion | bytes 131072 | tf_op jit(solution)/shard_map/slice | solution.py:327

commit v5 on v4

--- a/solution.py
+++ b/solution.py
@@ -212,7 +212,7 @@
 
     def deepen(t, g):
         with scope(f"L2_{t}{g}"):
-            for block in BLOCKS[6:]:
+            for block in ((0, 3), (0, 5), (1, 1), (1, 7), (1, 2), (1, 6), (0, 4), (1, 3), (1, 5), (1, 4)):
                 take(t, g, block)
 
     def work(t, g, chunk):
@@ -270,8 +270,8 @@
         leaf(t, 1, 0)
         leaf(t, 1, 1)
         relay(t, 0)
+        close(t, 0)
         relay(t, 1)
-        close(t, 0)
         if t + 1 < TICKS:
             enter(t + 1, 0)
         close(t, 1)

time: 82.4 us -> 83 us (level)
  Pallas kernels: 79.7 us -> 80.8 us
    pallas_call x1, Pallas kernels: 79.7 us -> 80.8 us  [on_device(): pl.pallas_call(functools.partial(kernel, n_pipe), out_shape=jax.ShapeDtyp...]
where the time goes in v5:
time: 83 us; the launch traced here: 82.8 us
  Pallas kernels  80.8 us (97%)
  local copies, waits for them, and re-layouts  1.4 us (2%)
    pallas_call x1, Pallas kernels, on_device(): pl.pallas_call(functools.partial(kernel, n_pipe), out_shape=jax.ShapeDtyp...  80.8 us

profile of v5, /device:TPU:6, one launch (start us, length us, event | category | flops | bytes accessed | tf_op | source)
XLA Modules:
  0.0 82.8 jit_solution(3405171890854199297)
XLA Ops:
  0.6 80.8 %shard_map.95 = bf16[2,8,2048]{2,1,0:T(8,128)(2,1)} custom-call(bf16[1,8,2048]{2,1,0:T(8,128)(2,1)} %down_ref.1, bf16[1,8,2048]{2,1,0:T(8,128)(2,1)} %up_ref.1, bf16[2,8,2048]{2,1,0:T(8,128)(2,1)} %feeds_ref.1, s32[2]{0:T(128)} %order_hbm.1, f32[1,2,2048]{2,1,0:T(2,128)} %gains_ref.1, bf16[1,2,2048,128]{3,2,1,0:T(8,128)(2,1)} %gate_ref.1, ...), custom_call_target="tpu_custom_call" | custom-call | tf_op jit(solution)/shard_map/pallas_call | solution.py:299
  81.4 1.4 %fusion = (bf16[1,8,2048]{2,1,0:T(8,128)(2,1)}, bf16[1,8,2048]{2,1,0:T(8,128)(2,1)}) fusion(bf16[2,8,2048]{2,1,0:T(8,128)(2,1)} %shard_map.95), kind=kLoop, calls=%fused_computation | loop fusion | bytes 131072 | tf_op jit(solution)/shard_map/slice | solution.py:327
